TPU v7x, 32 devices: a whole 2x2x4 slice. The times are simulated.
32 devices in a mesh: grp: 2 (over y), tile: 16 (over z, x, core).
Axes of the slice: x: 2, y: 2, z: 4, core: 2. Of those that a mesh axis runs over, the one named last changes fastest.
Arguments:
- fields: bfloat16 [6, 128, 128, 256], P('grp', 'tile'), parts along dimension 0, may hold values from -6 to 6
- seam_tile: int32 [3, 16, 2], P(None, 'tile'), may hold values from 0 to 47, as said below
- seam_code: int32 [3, 16, 2], P(None, 'tile'), may hold values from 0 to 3
- encoder_weight: bfloat16 [3, 3, 256, 256], replicated, may hold values from -0.125 to 0.125
- encoder_bias: float32 [256], replicated, may hold values from -3 to 3
- middle_weight: bfloat16 [3, 3, 256, 256], replicated, may hold values from -0.125 to 0.125
- middle_bias: float32 [256], replicated, may hold values from -3 to 3
- upconv_weight: bfloat16 [2, 2, 256, 256], replicated, may hold values from -0.375 to 0.375
- upconv_bias: float32 [256], replicated, may hold values from -3 to 3
- decoder_weight: bfloat16 [3, 3, 512, 256], replicated, may hold values from -0.09375 to 0.09375
- decoder_offset_bias: float32 [256], replicated, may hold values from -3 to 3
Outputs:
- decoded: bfloat16 [6, 128, 128, 256], P('grp', 'tile'), parts along dimension 0
There are 2 independent parts, one for each index of `grp`. A program takes and returns all parts, laid end to end along the dimension named above; an argument that names none is the same for every part. Nothing has to cross between parts.
Inputs may be any that keep to these rules, and one draw needn't show every extreme that they name: `seam_tile`: for each side, the 12 faces (cycle, face) name 12 different partner faces; all 4 tiles of one face side share the partner face and the code, and strip s names the tile of strip s of the partner face, or of strip 4 - 1 - s where the code is 2 or more.
All inputs are finite; a program needn't handle non-finite values.
Results may differ from a plain program's by a relative error of at most 0.0048.
Values may be sent and summed in bfloat16 or wider, within the bound.
A program may use at most 128 MiB of HBM per device.

v0:
```python
import functools

import jax
import jax.numpy as jnp
from jax import lax
from jax.experimental import pallas as pl
from jax.experimental.pallas import tpu as pltpu
from jax.sharding import PartitionSpec as P

F32 = jnp.float32
BF16 = jnp.bfloat16
FACES = 4


def gelu_tanh(x):
    return 0.5 * x * (1.0 + jnp.tanh(0.7978845608 * (x + 0.044715 * (x * x * x))))


def kernel(
    tiles,
    seam_tile,
    seam_code,
    fields_hbm,
    enc_w_hbm,
    mid_w_hbm,
    up_w_hbm,
    dec_w_hbm,
    enc_b,
    mid_b,
    up_b,
    dec_b,
    out,
    fields,
    enc_w,
    mid_w,
    up_w,
    dec_w,
    x_enc,
    x_skip,
    x_pool,
    x_up,
    acc_enc,
    acc_dec,
    coarse,
    fine,
    pair,
    corner_tmp,
    edge_tmp,
    seam_tmp,
    corner_src,
    corner_dst,
    corners,
    halo,
    halo_pool,
    edges,
    edges_pool,
    recv_enc,
    recv_skip,
    recv_up,
    recv_pool,
    corner_enc,
    corner_pool,
    corner_skip,
    corner_up,
    load_sem,
    send_sem,
    recv_sem,
):
    recv_corners = (corner_enc, corner_pool, corner_skip, corner_up)
    cycles, h, cols, ch = fields.shape
    hc, cc = h // 2, cols // 2
    strips = tiles // FACES
    me = lax.axis_index("tile")
    place = lax.rem(me + strips // 2, tiles)
    face = place // strips
    strip = place - face * strips
    top_face = strip == 0
    bottom_face = strip == strips - 1
    up_tile = lax.rem(me + tiles - 1, tiles)
    down_tile = lax.rem(me + 1, tiles)

    def tile_of(f, s):
        return lax.rem(f * strips + s + tiles - strips // 2, tiles)

    peers = []
    for kind in range(2):
        s = strip if kind == 0 else strips - 1 - strip
        for j in range(1 - kind, FACES):
            f = lax.rem(face + j, FACES)
            peers.append((kind, f, tile_of(f, s)))

    loads = []
    for k, (src, dst) in enumerate(
        ((fields_hbm, fields), (enc_w_hbm, enc_w), (dec_w_hbm, dec_w), (mid_w_hbm, mid_w), (up_w_hbm, up_w))
    ):
        copy = pltpu.make_async_copy(src, dst, load_sem.at[k])
        copy.start()
        loads.append(copy)

    barrier = pltpu.get_barrier_semaphore()
    targets = [up_tile, down_tile] + [peer for _, _, peer in peers]
    for target in targets:
        pl.semaphore_signal(barrier, inc=1, device_id={"tile": target})

    def remote(src, dst, e, send_at, recv_at, target):
        return pltpu.make_async_remote_copy(
            src_ref=src,
            dst_ref=dst,
            send_sem=send_sem.at[e, send_at],
            recv_sem=recv_sem.at[e, recv_at],
            device_id={"tile": target},
        )

    def spread(x, i, r, value):
        width = value.shape[0]
        at = lax.broadcasted_iota(jnp.int32, value.shape, 0)
        left = jnp.where(at == 0, 0.0, pltpu.roll(value, 1, 0))
        right = jnp.where(at == width - 1, 0.0, pltpu.roll(value, width - 1, 0))
        x[i, r, :, 0:ch] = left.astype(BF16)
        x[i, r, :, ch : 2 * ch] = value.astype(BF16)
        x[i, r, :, 2 * ch : 3 * ch] = right.astype(BF16)

    class Exchange:
        def __init__(self, e, x, halo_ref, edge_ref, recv_ref, source=None):
            self.e, self.x, self.halo, self.edges, self.recv = e, x, halo_ref, edge_ref, recv_ref
            self.rows = x.shape[0] - 2
            self.width = x.shape[2]
            self.source = source

        def row(self, i):
            if self.source is None:
                return self.x.at[i + 1, :, :, ch : 2 * ch]
            return self.source.at[:, i]

        def end_pixels(self, i, r):
            row = self.row(i)
            head = row[r, 0:16, :].astype(F32)[0:1]
            tail = row[r, self.width - 16 : self.width, :].astype(F32)[15:16]
            return head, tail

        def prepare(self):
            e, rows = self.e, self.rows
            for r in range(cycles):
                for i in range(rows):
                    for side, pixel in enumerate(self.end_pixels(i, r)):
                        k = 2 * r + side
                        edge_tmp[e, k, i : i + 1, :] = pixel
                        if i == 0:
                            corner_tmp[e, 0, k : k + 1, :] = pixel
                        if i == rows - 1:
                            corner_tmp[e, 1, k : k + 1, :] = pixel
            for which in range(2):
                corner_src[e, which] = corner_tmp[e, which].astype(BF16)
            value = edge_tmp[e, :, 0:rows, :].astype(BF16)
            self.edges[...] = value
            self.recv[face] = value

        def send(self):
            e, rows = self.e, self.rows
            self.copies = [
                remote(corner_src.at[e, 1], corner_dst.at[e, 0], e, 0, 0, down_tile),
                remote(corner_src.at[e, 0], corner_dst.at[e, 1], e, 1, 1, up_tile),
                remote(self.row(rows - 1), self.halo.at[0], e, 2, 2, down_tile),
                remote(self.row(0), self.halo.at[1], e, 3, 3, up_tile),
            ]
            self.seams = [
                remote(
                    self.edges,
                    self.recv.at[kind * FACES + face],
                    e,
                    4 + kind * FACES + f,
                    4 + kind * FACES + face,
                    peer,
                )
                for kind, f, peer in peers
            ]
            for copy in self.copies[0:2] + self.seams + self.copies[2:4]:
                copy.start()

        def relay(self):
            e = self.e
            self.copies[0].wait_recv()
            self.copies[1].wait_recv()
            above = jnp.where(top_face, 0.0, corner_dst[e, 0].astype(F32))
            below = jnp.where(bottom_face, 0.0, corner_dst[e, 1].astype(F32))
            value = jnp.concatenate([above, below], axis=0).astype(BF16)
            corners[e] = value
            self.recv_corner = recv_corners[e]
            self.recv_corner[face] = value
            self.relays = [
                remote(
                    corners.at[e],
                    self.recv_corner.at[kind * FACES + face],
                    e,
                    12 + kind * FACES + f,
                    12 + kind * FACES + face,
                    peer,
                )
                for kind, f, peer in peers
            ]
            for copy in self.relays:
                copy.start()

        def wait_rows(self):
            self.copies[2].wait_recv()
            self.copies[3].wait_recv()
            for r in range(cycles):
                above = jnp.where(top_face, 0.0, self.halo[0, r].astype(F32))
                spread(self.x, 0, r, above)
                below = jnp.where(bottom_face, 0.0, self.halo[1, r].astype(F32))
                spread(self.x, self.rows + 1, r, below)

        def wait_seams(self):
            e = self.e
            for kind, f, peer in peers:
                slot = kind * FACES + f
                remote(self.edges, self.recv.at[slot], e, 4 + slot, 4 + slot, peer).wait_recv()
                remote(
                    corners.at[e], self.recv_corner.at[slot], e, 12 + slot, 12 + slot, peer
                ).wait_recv()
            for copy in self.copies + self.seams + self.relays:
                copy.wait_send()

        def load_seams(self):
            rows = self.rows
            at = lax.broadcasted_iota(jnp.int32, (8, ch), 0)
            for side in range(2):
                for r in range(cycles):
                    partner, code = seam_tile[r, side], seam_code[r, side]
                    cycle = partner // tiles
                    home = lax.rem(partner - cycle * tiles + strips // 2, tiles) // strips
                    mirrored = code >= 2
                    slot = jnp.where(mirrored, FACES, 0) + home
                    k = 2 * cycle + lax.rem(code, 2)
                    column = self.recv[slot, k].astype(F32)
                    ends = self.recv_corner[slot].astype(F32)
                    above = jnp.sum(jnp.where(at == k, ends[0:8], 0.0), axis=0, keepdims=True)
                    below = jnp.sum(jnp.where(at == k, ends[8:16], 0.0), axis=0, keepdims=True)
                    seam_tmp[side, r, 0:1, :] = jnp.where(mirrored, below, above)
                    seam_tmp[side, r, rows + 1 : rows + 2, :] = jnp.where(mirrored, above, below)
                    for i in range(rows):
                        seam_tmp[side, r, i + 1 : i + 2, :] = jnp.where(
                            mirrored, column[rows - 1 - i : rows - i], column[i : i + 1]
                        )

        def add_seams(self, acc, weight_of):
            self.wait_seams()
            self.load_seams()
            for side in range(2):
                j = 0 if side == 0 else self.width - 1
                term = jnp.zeros((8 * cycles, ch), F32)
                for a in range(3):
                    tap = jnp.concatenate([seam_tmp[side, r, a : a + 8, :] for r in range(cycles)], axis=0)
                    term = term + jnp.dot(tap.astype(BF16), weight_of(a, 2 * side), preferred_element_type=F32)
                for r in range(cycles):
                    for i in range(self.rows):
                        acc[i, r, j : j + 1, :] += term[8 * r + i : 8 * r + i + 1]

    def conv_rows(x, start, count, weights):
        width = x.shape[2]
        taps = [x[pl.ds(start + a, count)].reshape(count * cycles * width, 3 * ch) for a in range(3)]
        product = jnp.dot(jnp.concatenate(taps, axis=1), weights(), preferred_element_type=F32)
        return product.reshape(count, cycles, width, ch)

    def enc_weights():
        return enc_w[...].reshape(9 * ch, ch)

    def mid_weights():
        return mid_w[...].reshape(9 * ch, ch)

    def dec_weights(part):
        def get():
            picked = [dec_w[a, b, part * ch : (part + 1) * ch, :] for a in range(3) for b in range(3)]
            return jnp.concatenate(picked, axis=0)

        return get

    def dec_tap(part):
        return lambda a, b: dec_w[a, b, part * ch : (part + 1) * ch, :]

    loads[0].wait()
    enc = Exchange(0, x_enc, halo.at[0], edges.at[0], recv_enc, fields)
    enc.prepare()
    @pl.loop(0, h)
    def _(i):
        for r in range(cycles):
            spread(x_enc, i + 1, r, fields[r, i].astype(F32))

    pl.semaphore_wait(barrier, len(targets))
    enc.send()

    loads[1].wait()

    def inner_rows(x, acc, weights, lo, hi, add):
        @pl.loop(lo, hi)
        def _(k):
            start = 1 + 2 * k
            value = conv_rows(x, start, 2, weights)
            if add:
                acc[pl.ds(start, 2)] += value
            else:
                acc[pl.ds(start, 2)] = value

    inner = (h - 2) // 2

    def outer_rows(x, acc, weights, add):
        @pl.loop(0, 2)
        def _(k):
            i = k * (h - 1)
            value = conv_rows(x, i, 1, weights)
            if add:
                acc[pl.ds(i, 1)] += value
            else:
                acc[pl.ds(i, 1)] = value

    inner_rows(x_enc, acc_enc, enc_weights, 0, 1, False)
    enc.relay()
    inner_rows(x_enc, acc_enc, enc_weights, 1, inner, False)
    enc.wait_rows()
    outer_rows(x_enc, acc_enc, enc_weights, False)
    enc.add_seams(acc_enc, lambda a, b: enc_w[a, b])

    @pl.loop(0, hc)
    def _(q):
        for r in range(cycles):
            total = None
            for a in range(2):
                value = gelu_tanh(acc_enc[2 * q + a, r] + enc_b[...]).astype(BF16).astype(F32)
                spread(x_skip, 2 * q + a + 1, r, value)
                total = value if total is None else total + value
            halves = []
            for k in range(ch // 128):
                pair[r, k] = total[:, k * 128 : (k + 1) * 128]
                even = pair[r, k, pl.ds(0, cc, stride=2), :]
                odd = pair[r, k, pl.ds(1, cc, stride=2), :]
                halves.append((even + odd) * 0.25)
            spread(x_pool, q + 1, r, jnp.concatenate(halves, axis=1).astype(BF16).astype(F32))

    pool = Exchange(1, x_pool, halo_pool, edges_pool, recv_pool)
    skip = Exchange(2, x_skip, halo.at[1], edges.at[1], recv_skip)
    pool.prepare()
    pool.send()
    skip.prepare()
    loads[2].wait()
    inner_rows(x_skip, acc_dec, dec_weights(1), 0, 1, False)
    pool.relay()
    skip.send()
    inner_rows(x_skip, acc_dec, dec_weights(1), 1, inner, False)

    loads[3].wait()
    loads[4].wait()
    pool.wait_rows()

    acc_mid = acc_enc.at[0:hc, :, 0:cc, :]

    @pl.loop(0, hc // 2)
    def _(k):
        acc_enc[pl.ds(2 * k, 2), :, 0:cc, :] = conv_rows(x_pool, 2 * k, 2, mid_weights)

    skip.relay()
    pool.add_seams(acc_mid, lambda a, b: mid_w[a, b])

    @pl.loop(0, hc)
    def _(q):
        for r in range(cycles):
            value = gelu_tanh(acc_enc[q, r, 0:cc, :] + mid_b[...])
            coarse[q, r] = value.astype(BF16)

    @pl.loop(0, hc)
    def _(q):
        lhs = coarse[q].reshape(cycles * cc, ch)
        for a in range(2):
            for b in range(2):
                value = jnp.dot(lhs, up_w[a, b], preferred_element_type=F32) + up_b[...]
                for r in range(cycles):
                    for k in range(ch // 128):
                        fine[a, r, k, pl.ds(b, cc, stride=2), :] = value[
                            r * cc : (r + 1) * cc, k * 128 : (k + 1) * 128
                        ]
            for r in range(cycles):
                row = jnp.concatenate([fine[a, r, k] for k in range(ch // 128)], axis=1)
                spread(x_up, 2 * q + a + 1, r, row.astype(BF16).astype(F32))

    up = Exchange(3, x_up, halo.at[2], edges.at[2], recv_up)
    up.prepare()
    up.send()
    skip.wait_rows()
    outer_rows(x_skip, acc_dec, dec_weights(1), False)
    up.relay()
    inner_rows(x_up, acc_dec, dec_weights(0), 0, inner, True)
    skip.add_seams(acc_dec, dec_tap(1))
    up.wait_rows()
    outer_rows(x_up, acc_dec, dec_weights(0), True)
    up.add_seams(acc_dec, dec_tap(0))

    @pl.loop(0, h)
    def _(i):
        for r in range(cycles):
            out[r, i] = (acc_dec[i, r] + dec_b[...]).astype(BF16)


def solution(mesh):
    tiles = mesh.shape["tile"]

    def on_device(fields, seam_tile, seam_code, enc_w, enc_b, mid_w, mid_b, up_w, up_b, dec_w, dec_b):
        cycles, h, cols, ch = fields.shape
        hc, cc = h // 2, cols // 2
        vmem = pl.BlockSpec(memory_space=pltpu.VMEM)
        smem = pl.BlockSpec(memory_space=pltpu.SMEM)
        hbm = pl.BlockSpec(memory_space=pl.ANY)
        ends = 2 * cycles
        slots = 2 * FACES
        return pl.pallas_call(
            functools.partial(kernel, tiles),
            out_shape=jax.ShapeDtypeStruct(fields.shape, BF16),
            in_specs=[smem, smem] + [hbm] * 5 + [vmem] * 4,
            out_specs=vmem,
            scratch_shapes=[
                pltpu.VMEM(fields.shape, BF16),
                pltpu.VMEM(enc_w.shape, BF16),
                pltpu.VMEM(mid_w.shape, BF16),
                pltpu.VMEM(up_w.shape, BF16),
                pltpu.VMEM(dec_w.shape, BF16),
                pltpu.VMEM((h + 2, cycles, cols, 3 * ch), BF16),
                pltpu.VMEM((h + 2, cycles, cols, 3 * ch), BF16),
                pltpu.VMEM((hc + 2, cycles, cc, 3 * ch), BF16),
                pltpu.VMEM((h + 2, cycles, cols, 3 * ch), BF16),
                pltpu.VMEM((h, cycles, cols, ch), F32),
                pltpu.VMEM((h, cycles, cols, ch), F32),
                pltpu.VMEM((hc, cycles, cc, ch), BF16),
                pltpu.VMEM((2, cycles, ch // 128, cols, 128), F32),
                pltpu.VMEM((cycles, ch // 128, cols, 128), F32),
                pltpu.VMEM((4, 2, 8, ch), F32),
                pltpu.VMEM((4, ends, 8, ch), F32),
                pltpu.VMEM((2, cycles, 16, ch), F32),
                pltpu.VMEM((4, 2, 8, ch), BF16),
                pltpu.VMEM((4, 2, 8, ch), BF16),
                pltpu.VMEM((4, 16, ch), BF16),
                pltpu.VMEM((3, 2, cycles, cols, ch), BF16),
                pltpu.VMEM((2, cycles, cc, ch), BF16),
                pltpu.VMEM((3, ends, h, ch), BF16),
                pltpu.VMEM((ends, hc, ch), BF16),
                pltpu.VMEM((slots, ends, h, ch), BF16),
                pltpu.VMEM((slots, ends, h, ch), BF16),
                pltpu.VMEM((slots, ends, h, ch), BF16),
                pltpu.VMEM((slots, ends, hc, ch), BF16),
                pltpu.VMEM((slots, 16, ch), BF16),
                pltpu.VMEM((slots, 16, ch), BF16),
                pltpu.VMEM((slots, 16, ch), BF16),
                pltpu.VMEM((slots, 16, ch), BF16),
                pltpu.SemaphoreType.DMA((5,)),
                pltpu.SemaphoreType.DMA((4, 4 + 2 * slots)),
                pltpu.SemaphoreType.DMA((4, 4 + 2 * slots)),
            ],
            compiler_params=pltpu.CompilerParams(
                collective_id=0, has_side_effects=True, vmem_limit_bytes=60 * 1024 * 1024
            ),
        )(
            seam_tile.reshape(cycles, 2),
            seam_code.reshape(cycles, 2),
            fields,
            enc_w,
            mid_w,
            up_w,
            dec_w,
            enc_b.reshape(1, ch),
            mid_b.reshape(1, ch),
            up_b.reshape(1, ch),
            dec_b.reshape(1, ch),
        )

    return jax.shard_map(
        on_device,
        mesh=mesh,
        in_specs=(P("grp", "tile", None, None), P(None, "tile", None), P(None, "tile", None)) + (P(),) * 8,
        out_specs=P("grp", "tile", None, None),
        check_vma=False,
    )
```

profile of v0, /device:TPU:0, one launch (start us, length us, event | category | flops | bytes accessed | tf_op | source)
XLA Modules:
  0.0 51.2 jit_solution(13351546167521907058)
XLA Ops:
  0.0 1.3 %copy.12.seam_tile = s32[3,2]{1,0:T(4,128)} copy(s32[3,2]{0,1:T(2,128)} %bitcast.10) | data formatting | bytes 48 | tf_op jit(solution)/shard_map/reshape | solution.py:459
  1.3 1.3 %copy.13.seam_code = s32[3,2]{1,0:T(4,128)} copy(s32[3,2]{0,1:T(2,128)} %bitcast.11) | data formatting | bytes 48 | tf_op jit(solution)/shard_map/reshape | solution.py:460
  2.7 45.8 %shard_map.109 = bf16[3,8,128,256]{3,2,1,0:T(8,128)(2,1)} custom-call(s32[3,2]{1,0:T(4,128)} %copy.12.seam_tile, s32[3,2]{1,0:T(4,128)} %copy.13.seam_code, bf16[3,8,128,256]{3,2,1,0:T(8,128)(2,1)} %fields_hbm.1, bf16[3,3,256,256]{3,2,1,0:T(8,128)(2,1)} %enc_w_hbm.1, bf16[3,3,256,256]{3,2,1,0:T(8,128)(2,1)} %mid_w_hbm.1, bf16[2,2,256,256]{3,2,1,0:T(8,128)(2,1)} %up_w_hbm.1, ...), custom_call_target="tpu_custom_call" | custom-call | tf_op jit(solution)/shard_map/pallas_call | solution.py:413
  48.5 2.7 %copy.15 = bf16[3,8,128,256]{3,2,1,0:T(8,128)(2,1)} copy(bf16[3,8,128,256]{3,2,1,0:T(8,128)(2,1)} %shard_map.109) | data formatting | bytes 3145728
where the time goes:
time: 51.4 us; the launch traced here: 51.2 us
  Pallas kernels  45.8 us (89%)
  local copies, waits for them, and re-layouts  5.37 us (10%)
    pallas_call x1, Pallas kernels, on_device(): pl.pallas_call(functools.partial(kernel, tiles), out_shape=jax.ShapeDtype...  45.8 us
    unnamed x1, local copies, waits for them, and re-layouts  2.7 us
    reshape x1, local copies, waits for them, and re-layouts, on_device(): seam_tile.reshape(cycles, 2)  1.34 us
    reshape x1, local copies, waits for them, and re-layouts, on_device(): seam_code.reshape(cycles, 2)  1.33 us

commit v1 on v0

v1 whole, which is shorter than its diff:
```python
import functools

import jax
import jax.numpy as jnp
from jax import lax
from jax.experimental import pallas as pl
from jax.experimental.pallas import tpu as pltpu
from jax.sharding import PartitionSpec as P

F32 = jnp.float32
BF16 = jnp.bfloat16
FACES = 4
SUB = 16


def gelu_tanh(x):
    return 0.5 * x * (1.0 + jnp.tanh(0.7978845608 * (x + 0.044715 * (x * x * x))))


def kernel(
    tiles,
    seam_tile,
    seam_code,
    fields_hbm,
    enc_w_hbm,
    mid_w_hbm,
    up_w_hbm,
    dec_w_hbm,
    enc_b,
    mid_b,
    up_b,
    dec_b,
    out,
    fields,
    enc_w,
    mid_w,
    up_w,
    dec_w,
    x_enc,
    x_skip,
    x_pool,
    x_up,
    coarse,
    acc_dec,
    pre,
    pixels,
    terms,
    p_in,
    p_out,
    edge_tmp,
    corner_tmp,
    seam_tmp,
    corner_src,
    edges_enc,
    edges_pool,
    edges_skip,
    edges_coarse,
    recv_enc,
    recv_pool,
    recv_skip,
    recv_coarse,
    corner_enc,
    corner_pool,
    corner_skip,
    corner_coarse,
    load_sem,
    send_sem,
    recv_sem,
):
    recv_corners = (corner_enc, corner_pool, corner_skip, corner_coarse)
    cycles, h, cols, ch = fields.shape
    hc = h // 2
    planes = cols // SUB
    cplanes = planes // 2
    strips = tiles // FACES
    me = lax.axis_index("tile")
    place = lax.rem(me + strips // 2, tiles)
    face = place // strips
    strip = place - face * strips
    top_face = strip == 0
    bottom_face = strip == strips - 1
    has_above = strip > 0
    has_below = strip < strips - 1
    up_tile = lax.rem(me + tiles - 1, tiles)
    down_tile = lax.rem(me + 1, tiles)
    at_sub = lax.broadcasted_iota(jnp.int32, (SUB, ch), 0)

    def tile_of(f, s):
        return lax.rem(f * strips + s + tiles - strips // 2, tiles)

    faces = [lax.rem(face + j, FACES) for j in range(FACES)]

    loads = []
    for k, (src, dst) in enumerate(
        ((fields_hbm, fields), (enc_w_hbm, enc_w), (dec_w_hbm, dec_w), (mid_w_hbm, mid_w), (up_w_hbm, up_w))
    ):
        copy = pltpu.make_async_copy(src, dst, load_sem.at[k])
        copy.start()
        loads.append(copy)

    barrier = pltpu.get_barrier_semaphore()

    @pl.loop(1, tiles)
    def _(k):
        pl.semaphore_signal(barrier, inc=1, device_id={"tile": lax.rem(me + k, tiles)})

    def remote(src, dst, e, send_at, recv_at, target):
        return pltpu.make_async_remote_copy(
            src_ref=src,
            dst_ref=dst,
            send_sem=send_sem.at[e, send_at],
            recv_sem=recv_sem.at[e, recv_at],
            device_id={"tile": target},
        )

    def shifted(value, last):
        if last:
            return jnp.where(at_sub == SUB - 1, 0.0, pltpu.roll(value, SUB - 1, 0)).astype(BF16)
        return jnp.where(at_sub == 0, 0.0, pltpu.roll(value, 1, 0)).astype(BF16)

    class Exchange:
        def __init__(self, e, rows, edge_ref, recv_ref, top, bottom, above, below):
            self.e, self.rows, self.edges, self.recv = e, rows, edge_ref, recv_ref
            self.top, self.bottom, self.above, self.below = top, bottom, above, below

        def publish(self):
            e, rows = self.e, self.rows
            value = edge_tmp[e, :, 0:rows, :].astype(BF16)
            self.edges[...] = value
            self.recv[face] = value
            for k in range(2 * cycles):
                corner_tmp[e, 0, k : k + 1, :] = edge_tmp[e, k, 0:1, :]
                corner_tmp[e, 1, k : k + 1, :] = edge_tmp[e, k, rows - 1 : rows, :]
            for which in range(2):
                corner_src[e, which] = corner_tmp[e, which].astype(BF16)

            @pl.when(strip == strips // 2 - 1)
            def _():
                recv_corners[e][1, FACES + face] = corner_tmp[e, 1].astype(BF16)

            @pl.when(strip == strips // 2)
            def _():
                recv_corners[e][0, FACES + face] = corner_tmp[e, 0].astype(BF16)

        def seam_copies(self):
            copies = []
            for kind in range(2):
                s = strip if kind == 0 else strips - 1 - strip
                for f in faces[1 - kind :]:
                    at = 2 + kind * FACES
                    copies.append(
                        remote(
                            self.edges,
                            self.recv.at[kind * FACES + face],
                            self.e,
                            at + f,
                            at + face,
                            tile_of(f, s),
                        )
                    )
            return copies

        def corner_copies(self):
            groups = []
            for which, s, pos, kind, cond, own in (
                (1, strip + 1, 0, 0, has_below, None),
                (1, strips - 2 - strip, 1, 1, has_below, strip != strips // 2 - 1),
                (0, strip + strips - 1, 1, 0, has_above, None),
                (0, strips - strip, 0, 1, has_above, strip != strips // 2),
            ):
                slot = kind * FACES + face
                at = 10 + 8 * pos
                for j, f in enumerate(faces):
                    copy = remote(
                        corner_src.at[self.e, which],
                        recv_corners[self.e].at[pos, slot],
                        self.e,
                        at + kind * FACES + f,
                        at + slot,
                        lax.rem(tile_of(f, s) + (tiles - strips if which == 0 and kind == 0 else 0), tiles),
                    )
                    ok = cond
                    if j == 0 and own is not None:
                        ok = jnp.logical_and(cond, own)
                    groups.append((ok, copy))
            return groups

        def row_copies(self):
            return [
                (has_below, remote(self.bottom, self.above, self.e, 0, 0, down_tile)),
                (has_above, remote(self.top, self.below, self.e, 1, 1, up_tile)),
            ]

        def send_seams(self):
            for copy in self.seam_copies():
                copy.start()
            for cond, copy in self.corner_copies():
                pl.when(cond)(copy.start)

        def send_rows(self):
            for cond, copy in self.row_copies():
                pl.when(cond)(copy.start)

        def wait_sends(self):
            for copy in self.seam_copies():
                copy.wait_send()
            for cond, copy in self.row_copies() + self.corner_copies():
                pl.when(cond)(copy.wait_send)

        def wait_above(self):
            remote(self.bottom, self.above, self.e, 0, 0, down_tile).wait_recv()

        def wait_below(self):
            remote(self.top, self.below, self.e, 1, 1, up_tile).wait_recv()

        def wait_seams(self):
            e = self.e
            for kind in range(2):
                for f in faces[1 - kind :]:
                    slot = kind * FACES + f
                    remote(self.edges, self.recv.at[slot], e, 2 + slot, 2 + slot, up_tile).wait_recv()
            for pos, cond, mid in ((0, has_above, strips // 2), (1, has_below, strips // 2 - 1)):
                for kind in range(2):
                    for j, f in enumerate(faces):
                        slot = kind * FACES + f
                        at = 10 + 8 * pos + slot
                        ok = cond
                        if j == 0 and kind == 1:
                            ok = jnp.logical_and(cond, strip != mid)
                        copy = remote(corner_src.at[e, 0], recv_corners[e].at[pos, slot], e, at, at, up_tile)
                        pl.when(ok)(copy.wait_recv)

        def load_seams(self):
            rows, e = self.rows, self.e
            at = lax.broadcasted_iota(jnp.int32, (8, ch), 0)
            for side in range(2):
                for r in range(cycles):
                    partner, code = seam_tile[side, r], seam_code[side, r]
                    cycle = partner // tiles
                    home = lax.rem(partner - cycle * tiles + strips // 2, tiles) // strips
                    mirrored = code >= 2
                    slot = jnp.where(mirrored, FACES, 0) + home
                    k = 2 * cycle + lax.rem(code, 2)
                    column = self.recv[slot, k].astype(F32)
                    ends = [recv_corners[e][pos, slot].astype(F32) for pos in range(2)]
                    above, below = [jnp.sum(jnp.where(at == k, end, 0.0), axis=0, keepdims=True) for end in ends]
                    seam_tmp[e, side, r, 0:1, :] = jnp.where(top_face, 0.0, above)
                    seam_tmp[e, side, r, rows + 1 : rows + 2, :] = jnp.where(bottom_face, 0.0, below)
                    for i in range(rows):
                        seam_tmp[e, side, r, i + 1 : i + 2, :] = jnp.where(
                            mirrored, column[rows - 1 - i : rows - i], column[i : i + 1]
                        )

    def seam_term(e, side, weight):
        lhs = [
            jnp.concatenate([seam_tmp[e, side, r, a : a + 8, :] for r in range(cycles)], axis=0) for a in range(3)
        ]
        return jnp.dot(jnp.concatenate(lhs, axis=1).astype(BF16), weight, preferred_element_type=F32)

    def conv(x, i, n, q, weight):
        taps = [
            x[pl.ds(i + a, n), b : b + q].reshape(n * q * cycles * SUB, ch) for a in range(3) for b in range(3)
        ]
        product = jnp.dot(jnp.concatenate(taps, axis=1), weight, preferred_element_type=F32)
        return product.reshape(n, q, cycles, SUB, ch)

    def keep_ends(stage, i, value):
        for r in range(cycles):
            pre[stage, 0, pl.ds(8 * r + i, 1), :] = value[0, r, 0:1, :]
            pre[stage, 1, pl.ds(8 * r + i, 1), :] = value[-1, r, SUB - 1 : SUB, :]

    def put_row(x, i, value):
        q = value.shape[0]
        x[i, 1 : q + 1] = value.astype(BF16)
        for r in range(cycles):
            x[i, 0, r] = shifted(value[q - 1, r], False)
            x[i, q + 1, r] = shifted(value[0, r], True)

    def halo_row(x, i, q, wait, missing):
        @pl.when(missing)
        def _():
            x[i] = jnp.zeros(x.shape[1:], BF16)

        @pl.when(jnp.logical_not(missing))
        def _():
            wait()
            for r in range(cycles):
                x[i, 0, r] = shifted(x[i, q, r].astype(F32), False)
                x[i, q + 1, r] = shifted(x[i, 1, r].astype(F32), True)

    def fix_ends(stage, ex, rows, term_of, tile_ref):
        for side in range(2):
            value = gelu_tanh(pre[stage, side] + term_of(side))
            pixels[side] = value
            for r in range(cycles):
                edge_tmp[ex.e, 2 * r + side, 0:rows, :] = value[8 * r : 8 * r + rows]
        for side in range(2):
            for r in range(cycles):
                for i in range(rows):
                    tile = tile_ref(i, side, r)
                    row = pixels[side, 8 * r + i : 8 * r + i + 1, :]
                    tile[...] = jnp.where(at_sub == side * (SUB - 1), row, tile[...].astype(F32)).astype(BF16)

    def steps(lo, hi, most, body):
        count = hi - lo
        unroll = max(u for u in range(1, most + 1) if count % u == 0)

        @pl.loop(0, count // unroll)
        def _(k):
            for u in range(unroll):
                body(lo + k * unroll + u)

    wide = (planes + 2) * SUB
    m = lax.broadcasted_iota(jnp.int32, (wide, cols), 0)
    j = lax.broadcasted_iota(jnp.int32, (wide, cols), 1)
    plane = m // SUB
    p_in[...] = jnp.where((m - plane * SUB) * planes + plane - 1 == j, 1.0, 0.0).astype(BF16)
    m = lax.broadcasted_iota(jnp.int32, (cols, cols), 0)
    j = lax.broadcasted_iota(jnp.int32, (cols, cols), 1)
    plane = j // SUB
    p_out[...] = jnp.where((j - plane * SUB) * planes + plane == m, 1.0, 0.0).astype(BF16)

    enc = Exchange(
        0, h, edges_enc, recv_enc, *[x_enc.at[i, 1 : planes + 1] for i in (1, h, 0, h + 1)]
    )
    pool = Exchange(
        1, hc, edges_pool, recv_pool, *[x_pool.at[i, 1 : cplanes + 1] for i in (1, hc, 0, hc + 1)]
    )
    skip = Exchange(
        2, h, edges_skip, recv_skip, *[x_skip.at[i, 1 : planes + 1] for i in (1, h, 0, h + 1)]
    )
    low = Exchange(3, hc, edges_coarse, recv_coarse, *[coarse.at[i] for i in (1, hc, 0, hc + 1)])

    loads[0].wait()
    for r in range(cycles):
        for i in range(h):
            edge_tmp[0, 2 * r, i : i + 1, :] = fields[r, i, 0:SUB, :].astype(F32)[0:1]
            edge_tmp[0, 2 * r + 1, i : i + 1, :] = fields[r, i, cols - SUB : cols, :].astype(F32)[SUB - 1 : SUB]
    enc.publish()

    def to_planes(i):
        for r in range(cycles):
            row = jnp.dot(p_in[...], fields[r, i], preferred_element_type=F32)
            x_enc[i + 1, :, r] = row.astype(BF16).reshape(planes + 2, SUB, ch)

    steps(0, h, 2, to_planes)
    pl.semaphore_wait(barrier, tiles - 1)
    enc.send_seams()
    enc.send_rows()

    loads[1].wait()

    def enc_row(i):
        value = conv(x_enc, i, 1, planes, enc_w[...].reshape(9 * ch, ch))[0] + enc_b[...]
        keep_ends(0, i, value)
        put_row(x_skip, i + 1, gelu_tanh(value))

    steps(1, h - 1, 3, enc_row)
    halo_row(x_enc, 0, planes, enc.wait_above, top_face)
    halo_row(x_enc, h + 1, planes, enc.wait_below, bottom_face)
    enc_row(0)
    enc_row(h - 1)
    enc.wait_seams()
    enc.load_seams()
    fix_ends(
        0,
        skip,
        h,
        lambda side: seam_term(0, side, enc_w[:, 2 * side].reshape(3 * ch, ch)),
        lambda i, side, r: x_skip.at[i + 1, planes if side else 1, r],
    )

    for q in range(hc):
        parts = []
        for k in range(cplanes):
            total = None
            for a in range(2):
                for b in range(2):
                    term = x_skip[2 * q + a + 1, 2 * k + b + 1].astype(F32)
                    total = term if total is None else total + term
            parts.append((total * 0.25)[None])
        value = jnp.concatenate(parts, axis=0)
        put_row(x_pool, q + 1, value)
        for r in range(cycles):
            edge_tmp[1, 2 * r, q : q + 1, :] = value[0, r, 0:1, :]
            edge_tmp[1, 2 * r + 1, q : q + 1, :] = value[-1, r, SUB - 1 : SUB, :]
    pool.publish()
    pool.send_seams()
    pool.send_rows()
    skip.publish()
    skip.send_seams()
    skip.send_rows()

    loads[2].wait()

    def dec_weights(part):
        picked = [dec_w[a, b, part * ch : (part + 1) * ch, :] for a in range(3) for b in range(3)]
        return jnp.concatenate(picked, axis=0)

    def dec_side(part, side):
        picked = [dec_w[a, 2 * side, part * ch : (part + 1) * ch, :] for a in range(3)]
        return jnp.concatenate(picked, axis=0)

    def dec_skip_row(i):
        acc_dec[i] = conv(x_skip, i, 1, planes, dec_weights(1))[0]

    steps(1, h - 1, 3, dec_skip_row)

    loads[3].wait()
    loads[4].wait()

    def mid_rows(i, n):
        value = conv(x_pool, i, n, cplanes, mid_w[...].reshape(9 * ch, ch)) + mid_b[...]
        for u in range(n):
            keep_ends(1, i + u, value[u])
        coarse[pl.ds(i + 1, n)] = gelu_tanh(value).astype(BF16)

    mid_rows(1, hc - 2)
    halo_row(x_pool, 0, cplanes, pool.wait_above, top_face)
    halo_row(x_pool, hc + 1, cplanes, pool.wait_below, bottom_face)
    mid_rows(0, 1)
    mid_rows(hc - 1, 1)
    pool.wait_seams()
    pool.load_seams()
    fix_ends(
        1,
        low,
        hc,
        lambda side: seam_term(1, side, mid_w[:, 2 * side].reshape(3 * ch, ch)),
        lambda i, side, r: coarse.at[i + 1, cplanes - 1 if side else 0, r],
    )
    low.publish()
    low.send_seams()
    low.send_rows()

    def up_rows(q, first, last):
        lhs = coarse[q].reshape(cplanes * cycles * SUB, ch)
        weight = jnp.concatenate([up_w[a, b] for a in range(first, last) for b in range(2)], axis=1)
        product = jnp.dot(lhs, weight, preferred_element_type=F32)
        for a in range(first, last):
            row = [None] * planes
            for b in range(2):
                at = (2 * (a - first) + b) * ch
                value = (product[:, at : at + ch] + up_b[...]).reshape(cplanes, cycles, SUB, ch)
                for k in range(cplanes):
                    row[2 * k + b] = value[k : k + 1]
            put_row(x_up, 2 * q + a - 1, jnp.concatenate(row, axis=0))

    for q in range(hc):
        up_rows(q + 1, 0, 2)

    def dec_up_row(i):
        value = acc_dec[i] + conv(x_up, i, 1, planes, dec_weights(0))[0] + dec_b[...]
        keep_ends(2, i, value)
        value = value.astype(BF16)
        for r in range(cycles):
            row = jnp.dot(p_out[...], value[:, r].reshape(cols, ch), preferred_element_type=F32)
            out[r, i] = row.astype(BF16)

    steps(1, h - 1, 3, dec_up_row)
    halo_row(x_skip, 0, planes, skip.wait_above, top_face)
    halo_row(x_skip, h + 1, planes, skip.wait_below, bottom_face)
    dec_skip_row(0)
    dec_skip_row(h - 1)
    skip.wait_seams()
    skip.load_seams()
    for side in range(2):
        terms[side] = seam_term(2, side, dec_side(1, side))

    for row, q, a, missing, wait in (
        (0, 0, 1, top_face, low.wait_above),
        (h + 1, hc + 1, 0, bottom_face, low.wait_below),
    ):

        @pl.when(missing)
        def _():
            x_up[row] = jnp.zeros(x_up.shape[1:], BF16)

        @pl.when(jnp.logical_not(missing))
        def _():
            wait()
            up_rows(q, a, a + 1)

    dec_up_row(0)
    dec_up_row(h - 1)

    low.wait_seams()
    low.load_seams()
    lhs = jnp.concatenate([seam_tmp[3, side, r, 0:8, :] for side in range(2) for r in range(cycles)], axis=0)
    weight = jnp.concatenate([up_w[a, b] for a in range(2) for b in range(2)], axis=1)
    product = jnp.dot(lhs.astype(BF16), weight, preferred_element_type=F32)
    for side in range(2):
        for r in range(cycles):
            code = seam_code[side, r]
            last = lax.rem(code, 2) == 1
            mirrored = code >= 2
            at = 8 * (side * cycles + r)
            phases = []
            for a in range(2):
                pair = [product[at : at + 8, (2 * a + b) * ch : (2 * a + b + 1) * ch] for b in range(2)]
                phases.append(jnp.where(last, pair[1], pair[0]) + up_b[...])
            even = jnp.where(mirrored, phases[1], phases[0])
            odd = jnp.where(mirrored, phases[0], phases[1])
            seam_tmp[4, side, r, 0:1, :] = jnp.where(top_face, 0.0, odd[0:1])
            for k in range(hc):
                seam_tmp[4, side, r, 2 * k + 1 : 2 * k + 2, :] = even[k + 1 : k + 2]
                seam_tmp[4, side, r, 2 * k + 2 : 2 * k + 3, :] = odd[k + 1 : k + 2]
            seam_tmp[4, side, r, h + 1 : h + 2, :] = jnp.where(bottom_face, 0.0, even[hc + 1 : hc + 2])
    for side in range(2):
        pixels[side] = pre[2, side] + terms[side] + seam_term(4, side, dec_side(0, side))
    for side in range(2):
        lo = side * (cols - SUB)
        for r in range(cycles):
            for i in range(h):
                row = pixels[side, 8 * r + i : 8 * r + i + 1, :]
                tile = out[r, i, lo : lo + SUB, :].astype(F32)
                out[r, i, lo : lo + SUB, :] = jnp.where(at_sub == side * (SUB - 1), row, tile).astype(BF16)

    for ex in (enc, pool, skip, low):
        ex.wait_sends()


def solution(mesh):
    tiles = mesh.shape["tile"]

    def on_device(fields, seam_tile, seam_code, enc_w, enc_b, mid_w, mid_b, up_w, up_b, dec_w, dec_b):
        cycles, h, cols, ch = fields.shape
        hc = h // 2
        planes = cols // SUB
        cplanes = planes // 2
        vmem = pl.BlockSpec(memory_space=pltpu.VMEM)
        smem = pl.BlockSpec(memory_space=pltpu.SMEM)
        hbm = pl.BlockSpec(memory_space=pl.ANY)
        ends = 2 * cycles
        slots = 2 * FACES
        return pl.pallas_call(
            functools.partial(kernel, tiles),
            out_shape=jax.ShapeDtypeStruct(fields.shape, BF16),
            in_specs=[smem, smem] + [hbm] * 5 + [vmem] * 4,
            out_specs=vmem,
            scratch_shapes=[
                pltpu.VMEM(fields.shape, BF16),
                pltpu.VMEM(enc_w.shape, BF16),
                pltpu.VMEM(mid_w.shape, BF16),
                pltpu.VMEM(up_w.shape, BF16),
                pltpu.VMEM(dec_w.shape, BF16),
                pltpu.VMEM((h + 2, planes + 2, cycles, SUB, ch), BF16),
                pltpu.VMEM((h + 2, planes + 2, cycles, SUB, ch), BF16),
                pltpu.VMEM((hc + 2, cplanes + 2, cycles, SUB, ch), BF16),
                pltpu.VMEM((h + 2, planes + 2, cycles, SUB, ch), BF16),
                pltpu.VMEM((hc + 2, cplanes, cycles, SUB, ch), BF16),
                pltpu.VMEM((h, planes, cycles, SUB, ch), F32),
                pltpu.VMEM((3, 2, 8 * cycles, ch), F32),
                pltpu.VMEM((2, 8 * cycles, ch), F32),
                pltpu.VMEM((2, 8 * cycles, ch), F32),
                pltpu.VMEM(((planes + 2) * SUB, cols), BF16),
                pltpu.VMEM((cols, cols), BF16),
                pltpu.VMEM((4, ends, 8, ch), F32),
                pltpu.VMEM((4, 2, 8, ch), F32),
                pltpu.VMEM((5, 2, cycles, 16, ch), F32),
                pltpu.VMEM((4, 2, 8, ch), BF16),
                pltpu.VMEM((ends, h, ch), BF16),
                pltpu.VMEM((ends, hc, ch), BF16),
                pltpu.VMEM((ends, h, ch), BF16),
                pltpu.VMEM((ends, hc, ch), BF16),
                pltpu.VMEM((slots, ends, h, ch), BF16),
                pltpu.VMEM((slots, ends, hc, ch), BF16),
                pltpu.VMEM((slots, ends, h, ch), BF16),
                pltpu.VMEM((slots, ends, hc, ch), BF16),
                pltpu.VMEM((2, slots, 8, ch), BF16),
                pltpu.VMEM((2, slots, 8, ch), BF16),
                pltpu.VMEM((2, slots, 8, ch), BF16),
                pltpu.VMEM((2, slots, 8, ch), BF16),
                pltpu.SemaphoreType.DMA((5,)),
                pltpu.SemaphoreType.DMA((4, 10 + 2 * slots)),
                pltpu.SemaphoreType.DMA((4, 10 + 2 * slots)),
            ],
            compiler_params=pltpu.CompilerParams(
                collective_id=0, has_side_effects=True, vmem_limit_bytes=60 * 1024 * 1024
            ),
        )(
            jnp.transpose(seam_tile, (1, 2, 0)).reshape(2, cycles),
            jnp.transpose(seam_code, (1, 2, 0)).reshape(2, cycles),
            fields,
            enc_w,
            mid_w,
            up_w,
            dec_w,
            enc_b.reshape(1, ch),
            mid_b.reshape(1, ch),
            up_b.reshape(1, ch),
            dec_b.reshape(1, ch),
        )

    return jax.shard_map(
        on_device,
        mesh=mesh,
        in_specs=(P("grp", "tile", None, None), P(None, "tile", None), P(None, "tile", None)) + (P(),) * 8,
        out_specs=P("grp", "tile", None, None),
        check_vma=False,
    )
```

time: 51.4 us -> 45 us (0.88)
  Pallas kernels: 45.8 us -> 42.1 us
  local copies, waits for them, and re-layouts: 5.37 us -> 2.7 us
    pallas_call x1, Pallas kernels: 45.8 us -> 42.1 us  [on_device(): pl.pallas_call(functools.partial(kernel, tiles), out_shape=jax.ShapeDtype...]
    reshape x2 -> x0, local copies, waits for them, and re-layouts: 2.66 us -> none  [the longest x1 1.34 us: on_device(): seam_tile.reshape(cycles, 2)]
where the time goes in v1:
time: 45 us; the launch traced here: 44.8 us
  Pallas kernels  42.1 us (94%)
  local copies, waits for them, and re-layouts  2.7 us (6%)
    pallas_call x1, Pallas kernels, on_device(): pl.pallas_call(functools.partial(kernel, tiles), out_shape=jax.ShapeDtype...  42.1 us
    unnamed x1, local copies, waits for them, and re-layouts  2.7 us

profile of v1, /device:TPU:0, one launch (start us, length us, event | category | flops | bytes accessed | tf_op | source)
XLA Modules:
  0.0 44.8 jit_solution(1726962682234353820)
XLA Ops:
  0.0 42.1 %shard_map.109 = bf16[3,8,128,256]{3,2,1,0:T(8,128)(2,1)} custom-call(s32[2,3]{1,0:T(2,128)} %bitcast.10, s32[2,3]{1,0:T(2,128)} %bitcast.11, bf16[3,8,128,256]{3,2,1,0:T(8,128)(2,1)} %fields_hbm.1, bf16[3,3,256,256]{3,2,1,0:T(8,128)(2,1)} %enc_w_hbm.1, bf16[3,3,256,256]{3,2,1,0:T(8,128)(2,1)} %mid_w_hbm.1, bf16[2,2,256,256]{3,2,1,0:T(8,128)(2,1)} %up_w_hbm.1, ...), custom_call_target="tpu_custom_call" | custom-call | tf_op jit(solution)/shard_map/pallas_call | solution.py:536
  42.1 2.7 %copy.13 = bf16[3,8,128,256]{3,2,1,0:T(8,128)(2,1)} copy(bf16[3,8,128,256]{3,2,1,0:T(8,128)(2,1)} %shard_map.109) | data formatting | bytes 3145728

commit v2 on v1

--- a/solution.py
+++ b/solution.py
@@ -81,6 +81,8 @@
     bottom_face = strip == strips - 1
     has_above = strip > 0
     has_below = strip < strips - 1
+    send_top = jnp.logical_and(has_above, strip != strips // 2)
+    send_bottom = jnp.logical_and(has_below, strip != strips // 2 - 1)
     up_tile = lax.rem(me + tiles - 1, tiles)
     down_tile = lax.rem(me + 1, tiles)
     at_sub = lax.broadcasted_iota(jnp.int32, (SUB, ch), 0)
@@ -134,56 +136,27 @@
             for which in range(2):
                 corner_src[e, which] = corner_tmp[e, which].astype(BF16)
 
-            @pl.when(strip == strips // 2 - 1)
-            def _():
-                recv_corners[e][1, FACES + face] = corner_tmp[e, 1].astype(BF16)
-
-            @pl.when(strip == strips // 2)
-            def _():
-                recv_corners[e][0, FACES + face] = corner_tmp[e, 0].astype(BF16)
-
-        def seam_copies(self):
-            copies = []
+        def send_seams(self):
+            e = self.e
             for kind in range(2):
                 s = strip if kind == 0 else strips - 1 - strip
                 for f in faces[1 - kind :]:
-                    at = 2 + kind * FACES
-                    copies.append(
-                        remote(
-                            self.edges,
-                            self.recv.at[kind * FACES + face],
-                            self.e,
-                            at + f,
-                            at + face,
-                            tile_of(f, s),
-                        )
-                    )
-            return copies
-
-        def corner_copies(self):
-            groups = []
-            for which, s, pos, kind, cond, own in (
-                (1, strip + 1, 0, 0, has_below, None),
-                (1, strips - 2 - strip, 1, 1, has_below, strip != strips // 2 - 1),
-                (0, strip + strips - 1, 1, 0, has_above, None),
-                (0, strips - strip, 0, 1, has_above, strip != strips // 2),
-            ):
-                slot = kind * FACES + face
-                at = 10 + 8 * pos
-                for j, f in enumerate(faces):
-                    copy = remote(
-                        corner_src.at[self.e, which],
-                        recv_corners[self.e].at[pos, slot],
-                        self.e,
-                        at + kind * FACES + f,
-                        at + slot,
-                        lax.rem(tile_of(f, s) + (tiles - strips if which == 0 and kind == 0 else 0), tiles),
-                    )
-                    ok = cond
-                    if j == 0 and own is not None:
-                        ok = jnp.logical_and(cond, own)
-                    groups.append((ok, copy))
-            return groups
+                    remote(self.edges, self.recv.at[kind * FACES + face], e, 2, 2, tile_of(f, s)).start()
+
+            def corner(which, pos, kind, s):
+                for f in faces:
+                    dst = recv_corners[e].at[pos, kind * FACES + face]
+                    remote(corner_src.at[e, which], dst, e, 3 + which, 3 + pos, tile_of(f, s)).start()
+
+            @pl.when(send_bottom)
+            def _():
+                corner(1, 0, 0, strip + 1)
+                corner(1, 1, 1, strips - 2 - strip)
+
+            @pl.when(send_top)
+            def _():
+                corner(0, 1, 0, strip - 1)
+                corner(0, 0, 1, strips - strip)
 
         def row_copies(self):
             return [
@@ -191,20 +164,23 @@
                 (has_above, remote(self.top, self.below, self.e, 1, 1, up_tile)),
             ]
 
-        def send_seams(self):
-            for copy in self.seam_copies():
-                copy.start()
-            for cond, copy in self.corner_copies():
-                pl.when(cond)(copy.start)
-
         def send_rows(self):
             for cond, copy in self.row_copies():
                 pl.when(cond)(copy.start)
 
+        def seam_wait(self):
+            others = self.recv.at[pl.ds(0, 2 * FACES - 1)]
+            return remote(others, others, self.e, 2, 2, up_tile)
+
+        def corner_wait(self, at):
+            whole = recv_corners[self.e].at[at]
+            return remote(whole, whole, self.e, 3 + at, 3 + at, up_tile)
+
         def wait_sends(self):
-            for copy in self.seam_copies():
-                copy.wait_send()
-            for cond, copy in self.row_copies() + self.corner_copies():
+            self.seam_wait().wait_send()
+            pl.when(send_top)(self.corner_wait(0).wait_send)
+            pl.when(send_bottom)(self.corner_wait(1).wait_send)
+            for cond, copy in self.row_copies():
                 pl.when(cond)(copy.wait_send)
 
         def wait_above(self):
@@ -214,21 +190,9 @@
             remote(self.top, self.below, self.e, 1, 1, up_tile).wait_recv()
 
         def wait_seams(self):
-            e = self.e
-            for kind in range(2):
-                for f in faces[1 - kind :]:
-                    slot = kind * FACES + f
-                    remote(self.edges, self.recv.at[slot], e, 2 + slot, 2 + slot, up_tile).wait_recv()
-            for pos, cond, mid in ((0, has_above, strips // 2), (1, has_below, strips // 2 - 1)):
-                for kind in range(2):
-                    for j, f in enumerate(faces):
-                        slot = kind * FACES + f
-                        at = 10 + 8 * pos + slot
-                        ok = cond
-                        if j == 0 and kind == 1:
-                            ok = jnp.logical_and(cond, strip != mid)
-                        copy = remote(corner_src.at[e, 0], recv_corners[e].at[pos, slot], e, at, at, up_tile)
-                        pl.when(ok)(copy.wait_recv)
+            self.seam_wait().wait_recv()
+            pl.when(jnp.logical_and(has_above, strip != strips // 2))(self.corner_wait(0).wait_recv)
+            pl.when(jnp.logical_and(has_below, strip != strips // 2 - 1))(self.corner_wait(1).wait_recv)
 
         def load_seams(self):
             rows, e = self.rows, self.e
@@ -242,8 +206,12 @@
                     slot = jnp.where(mirrored, FACES, 0) + home
                     k = 2 * cycle + lax.rem(code, 2)
                     column = self.recv[slot, k].astype(F32)
+                    twin = self.recv[jnp.where(mirrored, 0, FACES) + home, k].astype(F32)
+                    first, last = twin[0:1], twin[rows - 1 : rows]
                     ends = [recv_corners[e][pos, slot].astype(F32) for pos in range(2)]
                     above, below = [jnp.sum(jnp.where(at == k, end, 0.0), axis=0, keepdims=True) for end in ends]
+                    above = jnp.where(strip == strips // 2, jnp.where(mirrored, first, last), above)
+                    below = jnp.where(strip == strips // 2 - 1, jnp.where(mirrored, last, first), below)
                     seam_tmp[e, side, r, 0:1, :] = jnp.where(top_face, 0.0, above)
                     seam_tmp[e, side, r, rows + 1 : rows + 2, :] = jnp.where(bottom_face, 0.0, below)
                     for i in range(rows):
@@ -467,6 +435,8 @@
     for side in range(2):
         terms[side] = seam_term(2, side, dec_side(1, side))
 
+    for ex in (enc, pool, skip):
+        ex.wait_sends()
     for row, q, a, missing, wait in (
         (0, 0, 1, top_face, low.wait_above),
         (h + 1, hc + 1, 0, bottom_face, low.wait_below),
@@ -516,8 +486,7 @@
                 tile = out[r, i, lo : lo + SUB, :].astype(F32)
                 out[r, i, lo : lo + SUB, :] = jnp.where(at_sub == side * (SUB - 1), row, tile).astype(BF16)
 
-    for ex in (enc, pool, skip, low):
-        ex.wait_sends()
+    low.wait_sends()
 
 
 def solution(mesh):
@@ -572,8 +541,8 @@
                 pltpu.VMEM((2, slots, 8, ch), BF16),
                 pltpu.VMEM((2, slots, 8, ch), BF16),
                 pltpu.SemaphoreType.DMA((5,)),
-                pltpu.SemaphoreType.DMA((4, 10 + 2 * slots)),
-                pltpu.SemaphoreType.DMA((4, 10 + 2 * slots)),
+                pltpu.SemaphoreType.DMA((4, 5)),
+                pltpu.SemaphoreType.DMA((4, 5)),
             ],
             compiler_params=pltpu.CompilerParams(
                 collective_id=0, has_side_effects=True, vmem_limit_bytes=60 * 1024 * 1024

time: 45 us -> 42.4 us (0.942)
  Pallas kernels: 42.1 us -> 39.6 us
    pallas_call x1, Pallas kernels: 42.1 us -> 39.6 us  [on_device(): pl.pallas_call(functools.partial(kernel, tiles), out_shape=jax.ShapeDtype...]
where the time goes in v2:
time: 42.4 us; the launch traced here: 42.3 us
  Pallas kernels  39.6 us (93%)
  local copies, waits for them, and re-layouts  2.7 us (6%)
    pallas_call x1, Pallas kernels, on_device(): pl.pallas_call(functools.partial(kernel, tiles), out_shape=jax.ShapeDtype...  39.6 us
    unnamed x1, local copies, waits for them, and re-layouts  2.7 us

profile of v2, /device:TPU:0, one launch (start us, length us, event | category | flops | bytes accessed | tf_op | source)
XLA Modules:
  0.0 42.3 jit_solution(359101631535995178)
XLA Ops:
  0.0 39.6 %shard_map.109 = bf16[3,8,128,256]{3,2,1,0:T(8,128)(2,1)} custom-call(s32[2,3]{1,0:T(2,128)} %bitcast.10, s32[2,3]{1,0:T(2,128)} %bitcast.11, bf16[3,8,128,256]{3,2,1,0:T(8,128)(2,1)} %fields_hbm.1, bf16[3,3,256,256]{3,2,1,0:T(8,128)(2,1)} %enc_w_hbm.1, bf16[3,3,256,256]{3,2,1,0:T(8,128)(2,1)} %mid_w_hbm.1, bf16[2,2,256,256]{3,2,1,0:T(8,128)(2,1)} %up_w_hbm.1, ...), custom_call_target="tpu_custom_call" | custom-call | tf_op jit(solution)/shard_map/pallas_call | solution.py:505
  39.6 2.7 %copy.13 = bf16[3,8,128,256]{3,2,1,0:T(8,128)(2,1)} copy(bf16[3,8,128,256]{3,2,1,0:T(8,128)(2,1)} %shard_map.109) | data formatting | bytes 3145728

commit v3 on v2

--- a/solution.py
+++ b/solution.py
@@ -96,9 +96,8 @@
     for k, (src, dst) in enumerate(
         ((fields_hbm, fields), (enc_w_hbm, enc_w), (dec_w_hbm, dec_w), (mid_w_hbm, mid_w), (up_w_hbm, up_w))
     ):
-        copy = pltpu.make_async_copy(src, dst, load_sem.at[k])
-        copy.start()
-        loads.append(copy)
+        loads.append(pltpu.make_async_copy(src, dst, load_sem.at[k]))
+    loads[0].start()
 
     barrier = pltpu.get_barrier_semaphore()
 
@@ -300,6 +299,7 @@
     low = Exchange(3, hc, edges_coarse, recv_coarse, *[coarse.at[i] for i in (1, hc, 0, hc + 1)])
 
     loads[0].wait()
+    loads[1].start()
     for r in range(cycles):
         for i in range(h):
             edge_tmp[0, 2 * r, i : i + 1, :] = fields[r, i, 0:SUB, :].astype(F32)[0:1]
@@ -317,6 +317,8 @@
     enc.send_rows()
 
     loads[1].wait()
+    for copy in loads[2:]:
+        copy.start()
 
     def enc_row(i):
         value = conv(x_enc, i, 1, planes, enc_w[...].reshape(9 * ch, ch))[0] + enc_b[...]
@@ -355,24 +357,24 @@
     pool.publish()
     pool.send_seams()
     pool.send_rows()
+
+    loads[2].wait()
+
+    def dec_weights(part):
+        picked = [dec_w[a, b, part * ch : (part + 1) * ch, :] for a in range(3) for b in range(3)]
+        return jnp.concatenate(picked, axis=0)
+
+    def dec_side(part, side):
+        picked = [dec_w[a, 2 * side, part * ch : (part + 1) * ch, :] for a in range(3)]
+        return jnp.concatenate(picked, axis=0)
+
+    def dec_skip_row(i):
+        acc_dec[i] = conv(x_skip, i, 1, planes, dec_weights(1))[0]
+
+    steps(1, h - 1, 3, dec_skip_row)
     skip.publish()
     skip.send_seams()
     skip.send_rows()
-
-    loads[2].wait()
-
-    def dec_weights(part):
-        picked = [dec_w[a, b, part * ch : (part + 1) * ch, :] for a in range(3) for b in range(3)]
-        return jnp.concatenate(picked, axis=0)
-
-    def dec_side(part, side):
-        picked = [dec_w[a, 2 * side, part * ch : (part + 1) * ch, :] for a in range(3)]
-        return jnp.concatenate(picked, axis=0)
-
-    def dec_skip_row(i):
-        acc_dec[i] = conv(x_skip, i, 1, planes, dec_weights(1))[0]
-
-    steps(1, h - 1, 3, dec_skip_row)
 
     loads[3].wait()
     loads[4].wait()
@@ -502,6 +504,22 @@
         hbm = pl.BlockSpec(memory_space=pl.ANY)
         ends = 2 * cycles
         slots = 2 * FACES
+        operands = [
+            pltpu.with_memory_space_constraint(x, pltpu.HBM)
+            for x in (
+                jnp.transpose(seam_tile, (1, 2, 0)).reshape(2, cycles),
+                jnp.transpose(seam_code, (1, 2, 0)).reshape(2, cycles),
+                fields,
+                enc_w,
+                mid_w,
+                up_w,
+                dec_w,
+                enc_b.reshape(1, ch),
+                mid_b.reshape(1, ch),
+                up_b.reshape(1, ch),
+                dec_b.reshape(1, ch),
+            )
+        ]
         return pl.pallas_call(
             functools.partial(kernel, tiles),
             out_shape=jax.ShapeDtypeStruct(fields.shape, BF16),
@@ -545,21 +563,9 @@
                 pltpu.SemaphoreType.DMA((4, 5)),
             ],
             compiler_params=pltpu.CompilerParams(
-                collective_id=0, has_side_effects=True, vmem_limit_bytes=60 * 1024 * 1024
+                collective_id=0, has_side_effects=True, vmem_limit_bytes=44 * 1024 * 1024
             ),
-        )(
-            jnp.transpose(seam_tile, (1, 2, 0)).reshape(2, cycles),
-            jnp.transpose(seam_code, (1, 2, 0)).reshape(2, cycles),
-            fields,
-            enc_w,
-            mid_w,
-            up_w,
-            dec_w,
-            enc_b.reshape(1, ch),
-            mid_b.reshape(1, ch),
-            up_b.reshape(1, ch),
-            dec_b.reshape(1, ch),
-        )
+        )(*operands)
 
     return jax.shard_map(
         on_device,

time: 42.4 us -> 39 us (0.920)
  Pallas kernels: 39.6 us -> 37.7 us
  local copies, waits for them, and re-layouts: 2.7 us -> 1.15 us
    pallas_call x1, Pallas kernels: 39.6 us -> 37.7 us  [on_device(): pl.pallas_call(functools.partial(kernel, tiles), out_shape=jax.ShapeDtype...]
    unnamed x1, local copies, waits for them, and re-layouts: 2.7 us -> 1.15 us
where the time goes in v3:
time: 39 us; the launch traced here: 38.8 us
  Pallas kernels  37.7 us (97%)
  local copies, waits for them, and re-layouts  1.15 us (3%)
    pallas_call x1, Pallas kernels, on_device(): pl.pallas_call(functools.partial(kernel, tiles), out_shape=jax.ShapeDtype...  37.7 us
    unnamed x1, local copies, waits for them, and re-layouts  1.15 us

profile of v3, /device:TPU:0, one launch (start us, length us, event | category | flops | bytes accessed | tf_op | source)
XLA Modules:
  0.0 38.8 jit_solution(17555988015904828381)
XLA Ops:
  0.0 37.7 %shard_map.109 = bf16[3,8,128,256]{3,2,1,0:T(8,128)(2,1)S(1)} custom-call(s32[2,3]{1,0:T(2,128)} %bitcast.10, s32[2,3]{1,0:T(2,128)} %bitcast.11, bf16[3,8,128,256]{3,2,1,0:T(8,128)(2,1)} %fields_hbm.1, bf16[3,3,256,256]{3,2,1,0:T(8,128)(2,1)} %enc_w_hbm.1, bf16[3,3,256,256]{3,2,1,0:T(8,128)(2,1)} %mid_w_hbm.1, bf16[2,2,256,256]{3,2,1,0:T(8,128)(2,1)} %up_w_hbm.1, ...), custom_call_target="tpu_custom_call" | custom-call | tf_op jit(solution)/shard_map/pallas_call | solution.py:523
  37.7 1.1 %copy.13 = bf16[3,8,128,256]{3,2,1,0:T(8,128)(2,1)} copy(bf16[3,8,128,256]{3,2,1,0:T(8,128)(2,1)S(1)} %shard_map.109) | data formatting | bytes 3145728

commit v4 on v3

--- a/solution.py
+++ b/solution.py
@@ -11,6 +11,7 @@
 BF16 = jnp.bfloat16
 FACES = 4
 SUB = 16
+RELAYED = (0, 1, 2, 3)
 
 
 def gelu_tanh(x):
@@ -137,7 +138,7 @@
 
         def send_seams(self):
             e = self.e
-            for kind in range(2):
+            for kind in range(1 if e in RELAYED else 2):
                 s = strip if kind == 0 else strips - 1 - strip
                 for f in faces[1 - kind :]:
                     remote(self.edges, self.recv.at[kind * FACES + face], e, 2, 2, tile_of(f, s)).start()
@@ -168,8 +169,20 @@
                 pl.when(cond)(copy.start)
 
         def seam_wait(self):
-            others = self.recv.at[pl.ds(0, 2 * FACES - 1)]
+            others = self.recv.at[pl.ds(0, (FACES if self.e in RELAYED else 2 * FACES) - 1)]
             return remote(others, others, self.e, 2, 2, up_tile)
+
+        def relay_copy(self):
+            step = jnp.where(strip < strips // 2, FACES - 1, 1)
+            twin = tile_of(lax.rem(face + step, FACES), strips - 1 - strip)
+            return remote(
+                self.recv.at[pl.ds(0, FACES)], self.recv.at[pl.ds(FACES, FACES)], self.e, 5, 5, twin
+            )
+
+        def relay(self):
+            if self.e in RELAYED:
+                self.seam_wait().wait_recv()
+                self.relay_copy().start()
 
         def corner_wait(self, at):
             whole = recv_corners[self.e].at[at]
@@ -177,6 +190,8 @@
 
         def wait_sends(self):
             self.seam_wait().wait_send()
+            if self.e in RELAYED:
+                self.relay_copy().wait_send()
             pl.when(send_top)(self.corner_wait(0).wait_send)
             pl.when(send_bottom)(self.corner_wait(1).wait_send)
             for cond, copy in self.row_copies():
@@ -189,7 +204,10 @@
             remote(self.top, self.below, self.e, 1, 1, up_tile).wait_recv()
 
         def wait_seams(self):
-            self.seam_wait().wait_recv()
+            if self.e in RELAYED:
+                self.relay_copy().wait_recv()
+            else:
+                self.seam_wait().wait_recv()
             pl.when(jnp.logical_and(has_above, strip != strips // 2))(self.corner_wait(0).wait_recv)
             pl.when(jnp.logical_and(has_below, strip != strips // 2 - 1))(self.corner_wait(1).wait_recv)
 
@@ -326,6 +344,7 @@
         put_row(x_skip, i + 1, gelu_tanh(value))
 
     steps(1, h - 1, 3, enc_row)
+    enc.relay()
     halo_row(x_enc, 0, planes, enc.wait_above, top_face)
     halo_row(x_enc, h + 1, planes, enc.wait_below, bottom_face)
     enc_row(0)
@@ -372,6 +391,7 @@
         acc_dec[i] = conv(x_skip, i, 1, planes, dec_weights(1))[0]
 
     steps(1, h - 1, 3, dec_skip_row)
+    pool.relay()
     skip.publish()
     skip.send_seams()
     skip.send_rows()
@@ -403,6 +423,8 @@
     low.send_seams()
     low.send_rows()
 
+    skip.relay()
+
     def up_rows(q, first, last):
         lhs = coarse[q].reshape(cplanes * cycles * SUB, ch)
         weight = jnp.concatenate([up_w[a, b] for a in range(first, last) for b in range(2)], axis=1)
@@ -428,6 +450,7 @@
             out[r, i] = row.astype(BF16)
 
     steps(1, h - 1, 3, dec_up_row)
+    low.relay()
     halo_row(x_skip, 0, planes, skip.wait_above, top_face)
     halo_row(x_skip, h + 1, planes, skip.wait_below, bottom_face)
     dec_skip_row(0)
@@ -559,8 +582,8 @@
                 pltpu.VMEM((2, slots, 8, ch), BF16),
                 pltpu.VMEM((2, slots, 8, ch), BF16),
                 pltpu.SemaphoreType.DMA((5,)),
-                pltpu.SemaphoreType.DMA((4, 5)),
-                pltpu.SemaphoreType.DMA((4, 5)),
+                pltpu.SemaphoreType.DMA((4, 6)),
+                pltpu.SemaphoreType.DMA((4, 6)),
             ],
             compiler_params=pltpu.CompilerParams(
                 collective_id=0, has_side_effects=True, vmem_limit_bytes=44 * 1024 * 1024

time: 39 us -> 37.5 us (0.962)
  Pallas kernels: 37.7 us -> 36.2 us
    pallas_call x1, Pallas kernels: 37.7 us -> 36.2 us  [on_device(): pl.pallas_call(functools.partial(kernel, tiles), out_shape=jax.ShapeDtype...]
where the time goes in v4:
time: 37.5 us; the launch traced here: 37.4 us
  Pallas kernels  36.2 us (97%)
  local copies, waits for them, and re-layouts  1.15 us (3%)
    pallas_call x1, Pallas kernels, on_device(): pl.pallas_call(functools.partial(kernel, tiles), out_shape=jax.ShapeDtype...  36.2 us
    unnamed x1, local copies, waits for them, and re-layouts  1.15 us

profile of v4, /device:TPU:0, one launch (start us, length us, event | category | flops | bytes accessed | tf_op | source)
XLA Modules:
  0.0 37.4 jit_solution(4952707901420255441)
XLA Ops:
  0.0 36.2 %shard_map.109 = bf16[3,8,128,256]{3,2,1,0:T(8,128)(2,1)S(1)} custom-call(s32[2,3]{1,0:T(2,128)} %bitcast.10, s32[2,3]{1,0:T(2,128)} %bitcast.11, bf16[3,8,128,256]{3,2,1,0:T(8,128)(2,1)} %fields_hbm.1, bf16[3,3,256,256]{3,2,1,0:T(8,128)(2,1)} %enc_w_hbm.1, bf16[3,3,256,256]{3,2,1,0:T(8,128)(2,1)} %mid_w_hbm.1, bf16[2,2,256,256]{3,2,1,0:T(8,128)(2,1)} %up_w_hbm.1, ...), custom_call_target="tpu_custom_call" | custom-call | tf_op jit(solution)/shard_map/pallas_call | solution.py:546
  36.2 1.1 %copy.13 = bf16[3,8,128,256]{3,2,1,0:T(8,128)(2,1)} copy(bf16[3,8,128,256]{3,2,1,0:T(8,128)(2,1)S(1)} %shard_map.109) | data formatting | bytes 3145728
